TPU v7x, 32 devices: a whole 2x2x4 slice. The times are simulated.
32 devices in a mesh: segment: 8 (over z, x), tp: 4 (over y, core).
Axes of the slice: x: 2, y: 2, z: 4, core: 2. Of those that a mesh axis runs over, the one named last changes fastest.
Arguments:
- layer_inputs: bfloat16 [8, 2, 128, 2048], P('segment', None, 'tp'), may hold values from -100 to 100, as said below
- cotangent: bfloat16 [2, 2, 128, 2048], P(None, None, 'tp'), may hold values from -6 to 6
- gate_weight: bfloat16 [8, 2048, 4096], P('segment', None, 'tp'), may hold values from -1 to 1, as said below
- up_weight: bfloat16 [8, 2048, 4096], P('segment', None, 'tp'), may hold values from -1 to 1, as said below
- down_weight: bfloat16 [8, 4096, 2048], P('segment', 'tp'), may hold values from -1 to 1, as said below
- gate_momentum: float32 [8, 1024, 4096], P('segment', None, 'tp'), may hold values from -48 to 48
- up_momentum: float32 [8, 1024, 4096], P('segment', None, 'tp'), may hold values from -48 to 48
- down_momentum: float32 [8, 4096, 1024], P('segment', 'tp'), may hold values from -48 to 48
Outputs:
- input_gradient: bfloat16 [8, 2, 128, 2048], P('segment', None, 'tp')
- new_gate_momentum: float32 [8, 1024, 4096], P('segment', None, 'tp')
- new_up_momentum: float32 [8, 1024, 4096], P('segment', None, 'tp')
- new_down_momentum: float32 [8, 4096, 1024], P('segment', 'tp')
Inputs may be any that keep to these rules, and one draw needn't show every extreme that they name: `layer_inputs`: stored layer inputs, independent for every section and micro-batch. `gate_weight`: sections 2l and 2l + 1 hold equal copies of one layer's weights. `up_weight`: sections 2l and 2l + 1 hold equal copies of one layer's weights. `down_weight`: sections 2l and 2l + 1 hold equal copies of one layer's weights.
All inputs are finite; a program needn't handle non-finite values.
Results may differ from a plain program's by a relative error of at most 0.02.
Values may be sent and summed in bfloat16 or wider, within the bound.
A program may use at most 128 MiB of HBM per device.

v0:
```python
import jax
import jax.numpy as jnp
from jax import lax
from jax.sharding import PartitionSpec as P

epsilon = 1e-05
momentum_decay = 0.9


def passed_along(block, axis, distance):
    devices = range(lax.axis_size(axis))
    route = [(i - distance, i) for i in devices if i - distance in devices]
    return lax.ppermute(block, axis, route)


def partner(block, axis, distance):
    count = lax.axis_size(axis)
    route = []
    for low in range(count):
        high = low | 1 << distance
        if high != low and high < count:
            route += [(low, high), (high, low)]
    return lax.ppermute(block, axis, route)


def contract_last(left, right):
    return lax.dot_general(
        left, right, (((1,), (1,)), ((), ())), preferred_element_type=jnp.float32
    )


def contract_rows(left, right):
    return lax.dot_general(
        left, right, (((0,), (0,)), ((), ())), preferred_element_type=jnp.float32
    )


def rounded(values):
    return lax.optimization_barrier(values.astype(jnp.bfloat16)).astype(jnp.float32)


def project(rows, gate_w, up_w):
    gate = jnp.dot(rows, gate_w, preferred_element_type=jnp.float32)
    up = jnp.dot(rows, up_w, preferred_element_type=jnp.float32)
    return (gate, up)


def backward_factors(incoming_rows, gate, up, down_w):
    hidden_grad = contract_last(incoming_rows, down_w)
    sigma = jax.nn.sigmoid(gate)
    silu = gate * sigma
    hidden = (silu * up).astype(jnp.bfloat16)
    gate_grad = (hidden_grad * up * sigma * (1.0 + gate * (1.0 - sigma))).astype(jnp.bfloat16)
    up_grad = (hidden_grad * silu).astype(jnp.bfloat16)
    return (hidden, gate_grad, up_grad)


def owned(array, start, size, axis):
    return lax.dynamic_slice_in_dim(array, start, size, axis)


def shards(
    layer_inputs,
    cotangent,
    gate_weight,
    up_weight,
    down_weight,
    gate_momentum,
    up_momentum,
    down_momentum,
):
    segments = lax.axis_size("segment")
    depth = segments // 2
    segment = lax.axis_index("segment")
    direction = segment % 2
    lower = direction == 0
    position = segment // 2
    gate_w = gate_weight[0]
    up_w = up_weight[0]
    down_w = down_weight[0]
    inputs = layer_inputs[0].astype(jnp.float32)
    micro, rows_dev, width = inputs.shape
    half = width // 2
    hidden_dev = gate_w.shape[1]
    total_rows = rows_dev * lax.axis_size("tp")
    inverse_norm = lax.rsqrt(jnp.mean(inputs * inputs, axis=-1, keepdims=True) + epsilon)
    exact = inputs * inverse_norm
    normed = exact.astype(jnp.bfloat16)
    entry = lax.dynamic_index_in_dim(cotangent, direction, 0, keepdims=False)
    ticks = depth + micro - 1
    wide_store = jnp.zeros((micro, total_rows, width), jnp.bfloat16)
    narrow_store = jnp.zeros((micro, total_rows, hidden_dev), jnp.bfloat16)
    extra = (wide_store, narrow_store, narrow_store, narrow_store) + (wide_store,)

    def process(tick, received, state):
        outgoing, backs, extra = state
        index = tick - position
        active = (index >= 0) & (index < micro)
        slot = jnp.clip(index, 0, micro - 1)
        local_in = jnp.where(position == 0, entry[slot], received)
        incoming_rows = lax.all_gather(local_in, "tp", axis=0, tiled=True)
        full_rows = lax.all_gather(normed[slot], "tp", axis=0, tiled=True)

        def factors():
            gate, up = project(full_rows, gate_w, up_w)
            return backward_factors(incoming_rows, gate, up, down_w)

        def resting():
            blank = jnp.zeros((total_rows, hidden_dev), jnp.bfloat16)
            return (blank, blank, blank)

        hidden, gate_grad, up_grad = lax.cond(active, factors, resting)
        count = lax.axis_size("tp") * rows_dev

        def compute():
            return contract_last(gate_grad, gate_w) + contract_last(up_grad, up_w)

        def quiet():
            return jnp.zeros((count, width), jnp.float32)

        normed_grad = lax.psum_scatter(
            lax.cond(active, compute, quiet).astype(jnp.bfloat16),
            "tp",
            scatter_dimension=0,
            tiled=True,
        ).astype(jnp.float32)
        scale = inverse_norm[slot]
        base = exact[slot]
        back = local_in.astype(jnp.float32) + scale * (
            normed_grad - base * jnp.mean(normed_grad * base, axis=-1, keepdims=True)
        )
        back = back.astype(jnp.bfloat16)
        backs = lax.dynamic_update_index_in_dim(
            backs, jnp.where(active, back, backs[slot]), slot, 0
        )
        fresh = (incoming_rows, hidden, gate_grad, up_grad) + (full_rows,)
        extra = tuple(
            (
                lax.dynamic_update_index_in_dim(
                    store, jnp.where(active, item, store[slot]), slot, 0
                )
                for store, item in zip(extra, fresh)
            )
        )
        return (back, backs, extra)

    zero_rows = jnp.zeros((rows_dev, width), jnp.bfloat16)
    state = process(
        0, zero_rows, (zero_rows, jnp.zeros((micro, rows_dev, width), jnp.bfloat16), extra)
    )

    def advance(tick, state):
        received = passed_along(state[0], "segment", 2)
        return process(tick, received, state)

    outgoing, backs, extra = lax.fori_loop(1, ticks, advance, state)
    keep_start = jnp.where(lower, 0, half)
    send_start = half - keep_start
    flat_rows = micro * total_rows
    normed_all = extra[4]
    normed_flat = normed_all.reshape(flat_rows, width)
    incoming_flat = extra[0].reshape(flat_rows, width)
    hidden_flat = extra[1].reshape(flat_rows, hidden_dev)
    gate_flat = extra[2].reshape(flat_rows, hidden_dev)
    up_flat = extra[3].reshape(flat_rows, hidden_dev)
    arrived = partner(
        (
            owned(normed_flat, send_start, half, 1),
            owned(incoming_flat, send_start, half, 1),
            hidden_flat,
            gate_flat,
            up_flat,
        ),
        "segment",
        0,
    )
    normed_keep = owned(normed_flat, keep_start, half, 1)
    incoming_keep = owned(incoming_flat, keep_start, half, 1)
    gate_share = contract_rows(normed_keep, gate_flat) + rounded(
        contract_rows(arrived[0], arrived[3])
    )
    up_share = contract_rows(normed_keep, up_flat) + rounded(contract_rows(arrived[0], arrived[4]))
    down_share = contract_rows(hidden_flat, incoming_keep) + rounded(
        contract_rows(arrived[2], arrived[1])
    )
    new_gate = (momentum_decay * gate_momentum[0] + gate_share)[None]
    new_up = (momentum_decay * up_momentum[0] + up_share)[None]
    new_down = (momentum_decay * down_momentum[0] + down_share)[None]
    return (backs[None], new_gate, new_up, new_down)


def solution(mesh):
    return jax.shard_map(
        shards,
        mesh=mesh,
        in_specs=(
            P("segment", None, "tp", None),
            P(None, None, "tp", None),
            P("segment", None, "tp"),
            P("segment", None, "tp"),
            P("segment", "tp", None),
            P("segment", None, "tp"),
            P("segment", None, "tp"),
            P("segment", "tp", None),
        ),
        out_specs=(
            P("segment", None, "tp", None),
            P("segment", None, "tp"),
            P("segment", None, "tp"),
            P("segment", "tp", None),
        ),
        check_vma=False,
    )
```

profile of v0, /device:TPU:24, one launch (start us, length us, event | category | flops | bytes accessed | tf_op | source)
XLA Modules:
  0.0 393.4 jit_solution(2091443625812940769)
XLA Ops:
  11.2 7.2 %all-gather.1 = bf16[1,128,2048]{2,1,0:T(8,128)(2,1)S(1)} all-gather(bf16[1,32,2048]{2,1,0:T(8,128)(2,1)S(1)} %constant_dynamic-slice_fusion.10), channel_id=3, replica_groups=mesh['segment'=8,'tp'=4] {'tp'}, dimensions={1}, use_global_device_ids=true | all-gather | bytes 655360 | tf_op jit(solution)/shard_map/all_gather | solution.py:102
  19.4 7.3 %all-gather.2 = bf16[1,1,128,2048]{3,2,1,0:T(8,128)(2,1)S(1)} all-gather(bf16[1,1,32,2048]{3,2,1,0:T(8,128)(2,1)S(1)} %dynamic-slice_select_fusion), channel_id=4, replica_groups=mesh['segment'=8,'tp'=4] {'tp'}, dimensions={2}, use_global_device_ids=true | all-gather | bytes 655360 | tf_op jit(solution)/shard_map/all_gather | solution.py:101
  34.8 23.9 %reduce-scatter.3.cloned.1.call-done = bf16[32,2048]{1,0:T(8,128)(2,1)} async-done(((bf16[128,2048]{1,0:T(8,128)(2,1)}), bf16[32,2048]{1,0:T(8,128)(2,1)}) %reduce-scatter.3.cloned.1.call-update) | async-done | bytes 131088 | tf_op jit(solution)/shard_map/reduce_scatter | solution.py:121
  62.5 254.1 %while.26 = (s32[]{:T(128)}, bf16[32,2048]{1,0:T(8,128)(2,1)}, bf16[2,32,2048]{2,1,0:T(8,128)(2,1)}, bf16[2,128,2048]{2,1,0:T(8,128)(2,1)}, bf16[2,128,1024]{2,1...) while((s32[]{:T(128)}, bf16[32,2048]{1,0:T(8,128)(2,1)}, ...), condition=%wide.region_14.15_spmd, body=%wide.region_7.14_spmd.sunk | while | flops 2688548864 | bytes 97781288 | solution.py:156
  66.3 6.6 %all-gather.4 = bf16[1,128,2048]{2,1,0:T(8,128)(2,1)S(1)} all-gather(bf16[1,32,2048]{2,1,0:T(8,128)(2,1)S(1)} %constant_dynamic-slice_fusion.19), channel_id=2, replica_groups=mesh['segment'=8,'tp'=4] {'tp'}, dimensions={1}, use_global_device_ids=true | all-gather | bytes 655360 | tf_op jit(solution)/shard_map/while/body/eval_jaxpr/all_gather | solution.py:102
  79.4 7.3 %all_gather.25 = bf16[128,2048]{1,0:T(8,128)(2,1)S(1)} all-gather(bf16[32,2048]{1,0:T(8,128)(2,1)S(1)} %bitcast_select_fusion.8), channel_id=1, replica_groups=mesh['segment'=8,'tp'=4] {'tp'}, dimensions={0}, use_global_device_ids=true | all-gather | bytes 655360 | tf_op jit(solution)/shard_map/while/body/eval_jaxpr/all_gather | solution.py:101
  92.1 30.4 %reduce-scatter.5.cloned.1.call-done = bf16[32,2048]{1,0:T(8,128)(2,1)} async-done(((bf16[128,2048]{1,0:T(8,128)(2,1)}), bf16[32,2048]{1,0:T(8,128)(2,1)}) %reduce-scatter.5.cloned.1.call-update) | async-done | bytes 131088 | tf_op jit(solution)/shard_map/while/body/eval_jaxpr/reduce_scatter | solution.py:121
  129.4 6.6 %all-gather.4 = bf16[1,128,2048]{2,1,0:T(8,128)(2,1)S(1)} all-gather(bf16[1,32,2048]{2,1,0:T(8,128)(2,1)S(1)} %constant_dynamic-slice_fusion.19), channel_id=2, replica_groups=mesh['segment'=8,'tp'=4] {'tp'}, dimensions={1}, use_global_device_ids=true | all-gather | bytes 655360 | tf_op jit(solution)/shard_map/while/body/eval_jaxpr/all_gather | solution.py:102
  142.5 7.3 %all_gather.25 = bf16[128,2048]{1,0:T(8,128)(2,1)S(1)} all-gather(bf16[32,2048]{1,0:T(8,128)(2,1)S(1)} %bitcast_select_fusion.8), channel_id=1, replica_groups=mesh['segment'=8,'tp'=4] {'tp'}, dimensions={0}, use_global_device_ids=true | all-gather | bytes 655360 | tf_op jit(solution)/shard_map/while/body/eval_jaxpr/all_gather | solution.py:101
  155.2 31.4 %reduce-scatter.5.cloned.1.call-done = bf16[32,2048]{1,0:T(8,128)(2,1)} async-done(((bf16[128,2048]{1,0:T(8,128)(2,1)}), bf16[32,2048]{1,0:T(8,128)(2,1)}) %reduce-scatter.5.cloned.1.call-update) | async-done | bytes 131088 | tf_op jit(solution)/shard_map/while/body/eval_jaxpr/reduce_scatter | solution.py:121
  193.4 6.6 %all-gather.4 = bf16[1,128,2048]{2,1,0:T(8,128)(2,1)S(1)} all-gather(bf16[1,32,2048]{2,1,0:T(8,128)(2,1)S(1)} %constant_dynamic-slice_fusion.19), channel_id=2, replica_groups=mesh['segment'=8,'tp'=4] {'tp'}, dimensions={1}, use_global_device_ids=true | all-gather | bytes 655360 | tf_op jit(solution)/shard_map/while/body/eval_jaxpr/all_gather | solution.py:102
  206.5 7.3 %all_gather.25 = bf16[128,2048]{1,0:T(8,128)(2,1)S(1)} all-gather(bf16[32,2048]{1,0:T(8,128)(2,1)S(1)} %bitcast_select_fusion.8), channel_id=1, replica_groups=mesh['segment'=8,'tp'=4] {'tp'}, dimensions={0}, use_global_device_ids=true | all-gather | bytes 655360 | tf_op jit(solution)/shard_map/while/body/eval_jaxpr/all_gather | solution.py:101
  213.8 6.4 %conditional.8 = (bf16[128,1024]{1,0:T(8,128)(2,1)S(1)}, bf16[128,1024]{1,0:T(8,128)(2,1)S(1)}, bf16[128,1024]{1,0:T(8,128)(2,1)S(1)}) conditional(s32[]{:T(128)} %convert_element_type.162, () %tuple.89, (bf16[128,2048]{1,0:T(8,128)(2,1)S(1)}, bf16[2048,1024]{1,0:T(8,128)(2,1)}, bf16[2048,1024]{1,0:T(8,128)(2,1)}, bf16[128,2048]{1,0:T(8,128)(2,1)S(1)}, ...), branch_computations={%region_8.8_spmd, %region_9.9_spmd} | conditional | flops 1612578816 | bytes 50593872 | solution.py:112
  213.8 3.0 fusion.31
  220.9 5.4 %conditional.9 = (bf16[128,2048]{1,0:T(8,128)(2,1)S(1)}) conditional(s32[]{:T(128)} %convert_element_type.162, () %tuple.88, (bf16[128,1024]{1,0:T(8,128)(2,1)S(1)}, bf16[2048,1024]{1,0:T(8,128)(2,1)}, bf16[128,1024]{1,0:T(8,128)(2,1)S(1)}, bf16[2048,1024]{1,0:T(8,128)(2,1)}) %tuple.91), branch_computations={%region_10.10_spmd, %region_11.11_spmd} | conditional | flops 1074266112 | bytes 28311588 | solution.py:122
  220.9 3.8 fusion.33
  231.8 18.9 %reduce-scatter.5.cloned.1.call-done = bf16[32,2048]{1,0:T(8,128)(2,1)} async-done(((bf16[128,2048]{1,0:T(8,128)(2,1)}), bf16[32,2048]{1,0:T(8,128)(2,1)}) %reduce-scatter.5.cloned.1.call-update) | async-done | bytes 131088 | tf_op jit(solution)/shard_map/while/body/eval_jaxpr/reduce_scatter | solution.py:121
  257.5 6.6 %all-gather.4 = bf16[1,128,2048]{2,1,0:T(8,128)(2,1)S(1)} all-gather(bf16[1,32,2048]{2,1,0:T(8,128)(2,1)S(1)} %constant_dynamic-slice_fusion.19), channel_id=2, replica_groups=mesh['segment'=8,'tp'=4] {'tp'}, dimensions={1}, use_global_device_ids=true | all-gather | bytes 655360 | tf_op jit(solution)/shard_map/while/body/eval_jaxpr/all_gather | solution.py:102
  270.6 7.3 %all_gather.25 = bf16[128,2048]{1,0:T(8,128)(2,1)S(1)} all-gather(bf16[32,2048]{1,0:T(8,128)(2,1)S(1)} %bitcast_select_fusion.8), channel_id=1, replica_groups=mesh['segment'=8,'tp'=4] {'tp'}, dimensions={0}, use_global_device_ids=true | all-gather | bytes 655360 | tf_op jit(solution)/shard_map/while/body/eval_jaxpr/all_gather | solution.py:101
  277.9 6.4 %conditional.8 = (bf16[128,1024]{1,0:T(8,128)(2,1)S(1)}, bf16[128,1024]{1,0:T(8,128)(2,1)S(1)}, bf16[128,1024]{1,0:T(8,128)(2,1)S(1)}) conditional(s32[]{:T(128)} %convert_element_type.162, () %tuple.89, (bf16[128,2048]{1,0:T(8,128)(2,1)S(1)}, bf16[2048,1024]{1,0:T(8,128)(2,1)}, bf16[2048,1024]{1,0:T(8,128)(2,1)}, bf16[128,2048]{1,0:T(8,128)(2,1)S(1)}, ...), branch_computations={%region_8.8_spmd, %region_9.9_spmd} | conditional | flops 1612578816 | bytes 50593872 | solution.py:112
  277.9 3.0 fusion.31
  285.0 5.4 %conditional.9 = (bf16[128,2048]{1,0:T(8,128)(2,1)S(1)}) conditional(s32[]{:T(128)} %convert_element_type.162, () %tuple.88, (bf16[128,1024]{1,0:T(8,128)(2,1)S(1)}, bf16[2048,1024]{1,0:T(8,128)(2,1)}, bf16[128,1024]{1,0:T(8,128)(2,1)S(1)}, bf16[2048,1024]{1,0:T(8,128)(2,1)}) %tuple.91), branch_computations={%region_10.10_spmd, %region_11.11_spmd} | conditional | flops 1074266112 | bytes 28311588 | solution.py:122
  285.0 3.8 fusion.33
  293.0 2.1 bitcast_dynamic-update-slice_fusion.20
  295.9 17.6 %reduce-scatter.5.cloned.1.call-done = bf16[32,2048]{1,0:T(8,128)(2,1)} async-done(((bf16[128,2048]{1,0:T(8,128)(2,1)}), bf16[32,2048]{1,0:T(8,128)(2,1)}) %reduce-scatter.5.cloned.1.call-update) | async-done | bytes 131088 | tf_op jit(solution)/shard_map/while/body/eval_jaxpr/reduce_scatter | solution.py:121
  327.8 15.0 %collective-permute-done.1 = bf16[256,1024]{1,0:T(8,128)(2,1)S(1)} collective-permute-done((bf16[256,1024]{1,0:T(8,128)(2,1)S(1)}, bf16[256,1024]{1,0:T(8,128)(2,1)S(1)}, u32[]{:S(2)}, u32[]{:S(2)}) %collective-permute-start.1) | collective-permute-done | bytes 524320 | tf_op jit(solution)/shard_map/ppermute | solution.py:23
  343.6 10.5 %collective-permute-done.3 = bf16[256,1024]{1,0:T(8,128)(2,1)S(1)} collective-permute-done((bf16[256,1024]{1,0:T(8,128)(2,1)}, bf16[256,1024]{1,0:T(8,128)(2,1)S(1)}, u32[]{:S(2)}, u32[]{:S(2)}) %collective-permute-start.3) | collective-permute-done | bytes 524320 | tf_op jit(solution)/shard_map/ppermute | solution.py:23
  354.8 10.5 %collective-permute-done.4 = bf16[256,1024]{1,0:T(8,128)(2,1)S(1)} collective-permute-done((bf16[256,1024]{1,0:T(8,128)(2,1)}, bf16[256,1024]{1,0:T(8,128)(2,1)S(1)}, u32[]{:S(2)}, u32[]{:S(2)}) %collective-permute-start.4) | collective-permute-done | bytes 524320 | tf_op jit(solution)/shard_map/ppermute | solution.py:23
  365.3 9.9 %collective-permute-done.5 = bf16[256,1024]{1,0:T(8,128)(2,1)S(1)} collective-permute-done((bf16[256,1024]{1,0:T(8,128)(2,1)S(1)}, bf16[256,1024]{1,0:T(8,128)(2,1)S(1)}, u32[]{:S(2)}, u32[]{:S(2)}) %collective-permute-start.5) | collective-permute-done | bytes 524320 | tf_op jit(solution)/shard_map/ppermute | solution.py:23
  376.0 3.6 fusion.9
  379.6 3.6 fusion.8
  383.2 3.6 fusion.7
  (186 shorter events, 114.4 us)
Async XLA Ops:
  7.2 51.6 %reduce-scatter.3.cloned.1.call-start = ((), (), s32[]{:S(2)}) async-start(), calls=%async_computation.2 | async-start | bytes 655360 | tf_op jit(solution)/shard_map/reduce_scatter | solution.py:121
  26.7 1.1 copy-start.13
  27.0 0.8 copy-start.12
  33.7 1.0 copy-start.6
  62.5 60.1 %reduce-scatter.5.cloned.1.call-start = ((), (), s32[]{:S(2)}) async-start(), calls=%async_computation.3 | async-start | bytes 655360 | tf_op jit(solution)/shard_map/while/body/eval_jaxpr/reduce_scatter | solution.py:121
  62.5 16.0 %collective-permute-start = (bf16[32,2048]{1,0:T(8,128)(2,1)}, bf16[32,2048]{1,0:T(8,128)(2,1)S(1)}, u32[]{:S(2)}, u32[]{:S(2)}) collective-permute-start(bf16[32,2048]{1,0:T(8,128)(2,1)} %get-tuple-element.638), channel_id=1, source_target_pairs={{0,8},{4,12},{8,16},{12,20},{16,24},{20,28},{1,9},{5,13},{9,17},{1... | collective-permute-start | bytes 393224 | tf_op jit(solution)/shard_map/while/body/eval_jaxpr/ppermute | solution.py:13
  87.6 0.8 copy-start.4
  88.4 35.4 %copy-start.8 = (bf16[1,32,2048]{2,1,0:T(8,128)(2,1)S(1)}, bf16[1,32,2048]{2,1,0:T(8,128)(2,1)}, u32[]{:S(2)}) copy-start(bf16[1,32,2048]{2,1,0:T(8,128)(2,1)} %constant_dynamic-slice_fusion.18) | copy-start | bytes 393220 | tf_op jit(solution)/shard_map/while
  125.6 61.0 %reduce-scatter.5.cloned.1.call-start = ((), (), s32[]{:S(2)}) async-start(), calls=%async_computation.3 | async-start | bytes 655360 | tf_op jit(solution)/shard_map/while/body/eval_jaxpr/reduce_scatter | solution.py:121
  125.6 16.0 %collective-permute-start = (bf16[32,2048]{1,0:T(8,128)(2,1)}, bf16[32,2048]{1,0:T(8,128)(2,1)S(1)}, u32[]{:S(2)}, u32[]{:S(2)}) collective-permute-start(bf16[32,2048]{1,0:T(8,128)(2,1)} %get-tuple-element.638), channel_id=1, source_target_pairs={{0,8},{4,12},{8,16},{12,20},{16,24},{20,28},{1,9},{5,13},{9,17},{1... | collective-permute-start | bytes 393224 | tf_op jit(solution)/shard_map/while/body/eval_jaxpr/ppermute | solution.py:13
  151.5 36.3 %copy-start.8 = (bf16[1,32,2048]{2,1,0:T(8,128)(2,1)S(1)}, bf16[1,32,2048]{2,1,0:T(8,128)(2,1)}, u32[]{:S(2)}) copy-start(bf16[1,32,2048]{2,1,0:T(8,128)(2,1)} %constant_dynamic-slice_fusion.18) | copy-start | bytes 393220 | tf_op jit(solution)/shard_map/while
  189.6 61.1 %reduce-scatter.5.cloned.1.call-start = ((), (), s32[]{:S(2)}) async-start(), calls=%async_computation.3 | async-start | bytes 655360 | tf_op jit(solution)/shard_map/while/body/eval_jaxpr/reduce_scatter | solution.py:121
  189.6 16.0 %collective-permute-start = (bf16[32,2048]{1,0:T(8,128)(2,1)}, bf16[32,2048]{1,0:T(8,128)(2,1)S(1)}, u32[]{:S(2)}, u32[]{:S(2)}) collective-permute-start(bf16[32,2048]{1,0:T(8,128)(2,1)} %get-tuple-element.638), channel_id=1, source_target_pairs={{0,8},{4,12},{8,16},{12,20},{16,24},{20,28},{1,9},{5,13},{9,17},{1... | collective-permute-start | bytes 393224 | tf_op jit(solution)/shard_map/while/body/eval_jaxpr/ppermute | solution.py:13
  213.8 3.4 copy-start.2
  213.8 4.7 %copy-start.15 = (bf16[1024,2048]{1,0:T(8,128)(2,1)S(1)}, bf16[1024,2048]{1,0:T(8,128)(2,1)}, u32[]{:S(2)}) copy-start(bf16[1024,2048]{1,0:T(8,128)(2,1)} %get-tuple-element.369) | copy-start | bytes 12582916 | tf_op jit(solution)/shard_map/while/body/eval_jaxpr/cond
  220.9 3.9 copy-start.3
  227.1 24.7 %copy-start.8 = (bf16[1,32,2048]{2,1,0:T(8,128)(2,1)S(1)}, bf16[1,32,2048]{2,1,0:T(8,128)(2,1)}, u32[]{:S(2)}) copy-start(bf16[1,32,2048]{2,1,0:T(8,128)(2,1)} %constant_dynamic-slice_fusion.18) | copy-start | bytes 393220 | tf_op jit(solution)/shard_map/while
  253.7 59.8 %reduce-scatter.5.cloned.1.call-start = ((), (), s32[]{:S(2)}) async-start(), calls=%async_computation.3 | async-start | bytes 655360 | tf_op jit(solution)/shard_map/while/body/eval_jaxpr/reduce_scatter | solution.py:121
  253.7 16.0 %collective-permute-start = (bf16[32,2048]{1,0:T(8,128)(2,1)}, bf16[32,2048]{1,0:T(8,128)(2,1)S(1)}, u32[]{:S(2)}, u32[]{:S(2)}) collective-permute-start(bf16[32,2048]{1,0:T(8,128)(2,1)} %get-tuple-element.638), channel_id=1, source_target_pairs={{0,8},{4,12},{8,16},{12,20},{16,24},{20,28},{1,9},{5,13},{9,17},{1... | collective-permute-start | bytes 393224 | tf_op jit(solution)/shard_map/while/body/eval_jaxpr/ppermute | solution.py:13
  277.9 3.4 copy-start.2
  277.9 4.7 %copy-start.15 = (bf16[1024,2048]{1,0:T(8,128)(2,1)S(1)}, bf16[1024,2048]{1,0:T(8,128)(2,1)}, u32[]{:S(2)}) copy-start(bf16[1024,2048]{1,0:T(8,128)(2,1)} %get-tuple-element.369) | copy-start | bytes 12582916 | tf_op jit(solution)/shard_map/while/body/eval_jaxpr/cond
  285.0 3.9 copy-start.3
  291.2 23.5 %copy-start.8 = (bf16[1,32,2048]{2,1,0:T(8,128)(2,1)S(1)}, bf16[1,32,2048]{2,1,0:T(8,128)(2,1)}, u32[]{:S(2)}) copy-start(bf16[1,32,2048]{2,1,0:T(8,128)(2,1)} %constant_dynamic-slice_fusion.18) | copy-start | bytes 393220 | tf_op jit(solution)/shard_map/while
  316.6 26.2 %collective-permute-start.2 = (bf16[256,1024]{1,0:T(8,128)(2,1)}, bf16[256,1024]{1,0:T(8,128)(2,1)S(1)}, u32[]{:S(2)}, u32[]{:S(2)}) collective-permute-start(bf16[256,1024]{1,0:T(8,128)(2,1)} %bitcast.38), channel_id=1, source_target_pairs={{0,4},{4,0},{8,12},{12,8},{16,20},{20,16},{24,28},{28,24},{1,5},{5... | collective-permute-start | bytes 1572872 | tf_op jit(solution)/shard_map/ppermute | solution.py:23
  318.0 4.6 %copy-start.7 = (bf16[2,128,2048]{2,1,0:T(8,128)(2,1)S(1)}, bf16[2,128,2048]{2,1,0:T(8,128)(2,1)}, u32[]{:S(2)}) copy-start(bf16[2,128,2048]{2,1,0:T(8,128)(2,1)} %get-tuple-element.416) | copy-start | bytes 3145732
  320.0 22.8 %collective-permute-start.1 = (bf16[256,1024]{1,0:T(8,128)(2,1)S(1)}, bf16[256,1024]{1,0:T(8,128)(2,1)S(1)}, u32[]{:S(2)}, u32[]{:S(2)}) collective-permute-start(bf16[256,1024]{1,0:T(8,128)(2,1)S(1)} %constant_dynamic-slice_fusion.9), channel_id=1, source_target_pairs={{0,4},{4,0},{8,12},{12,8},{16,20},{20,16},{24,28},{28,24},{1,5},{5... | collective-permute-start | bytes 1572872 | tf_op jit(solution)/shard_map/ppermute | solution.py:23
  320.6 33.5 %collective-permute-start.3 = (bf16[256,1024]{1,0:T(8,128)(2,1)}, bf16[256,1024]{1,0:T(8,128)(2,1)S(1)}, u32[]{:S(2)}, u32[]{:S(2)}) collective-permute-start(bf16[256,1024]{1,0:T(8,128)(2,1)} %bitcast.41), channel_id=1, source_target_pairs={{0,4},{4,0},{8,12},{12,8},{16,20},{20,16},{24,28},{28,24},{1,5},{5... | collective-permute-start | bytes 1572872 | tf_op jit(solution)/shard_map/ppermute | solution.py:23
  322.1 43.2 %collective-permute-start.4 = (bf16[256,1024]{1,0:T(8,128)(2,1)}, bf16[256,1024]{1,0:T(8,128)(2,1)S(1)}, u32[]{:S(2)}, u32[]{:S(2)}) collective-permute-start(bf16[256,1024]{1,0:T(8,128)(2,1)} %bitcast.44), channel_id=1, source_target_pairs={{0,4},{4,0},{8,12},{12,8},{16,20},{20,16},{24,28},{28,24},{1,5},{5... | collective-permute-start | bytes 1572872 | tf_op jit(solution)/shard_map/ppermute | solution.py:23
  322.7 52.6 %collective-permute-start.5 = (bf16[256,1024]{1,0:T(8,128)(2,1)S(1)}, bf16[256,1024]{1,0:T(8,128)(2,1)S(1)}, u32[]{:S(2)}, u32[]{:S(2)}) collective-permute-start(bf16[256,1024]{1,0:T(8,128)(2,1)S(1)} %constant_dynamic-slice_fusion.8), channel_id=1, source_target_pairs={{0,4},{4,0},{8,12},{12,8},{16,20},{20,16},{24,28},{28,24},{1,5},{5... | collective-permute-start | bytes 1572872 | tf_op jit(solution)/shard_map/ppermute | solution.py:23
  327.8 48.2 %copy-start.9 = (f32[1,1024,1024]{2,1,0:T(8,128)S(1)}, f32[1,1024,1024]{2,1,0:T(8,128)}, u32[]{:S(2)}) copy-start(f32[1,1024,1024]{2,1,0:T(8,128)} %param.23) | copy-start | bytes 12582916
  376.0 3.6 copy-start.10
  379.6 3.6 copy-start.11
  (7 other events, 5.3 us)
Sparse Core Ops, SparseCore 0:
  27.9 30.7 reduce-scatter.2
  88.5 34.0 reduce-scatter.4
  151.6 34.9 reduce-scatter.4
  227.2 23.4 reduce-scatter.4
  291.3 22.2 reduce-scatter.4
where the time goes:
time: 397 us; the launch traced here: 393 us
  waiting for transfers between devices  168 us (42%)
  blocking collectives  70 us (18%)
  other arithmetic  53.3 us (13%)
  local copies, waits for them, and re-layouts  47 us (12%)
  matrix products  29.2 us (7%)
  between operations  13.9 us (4%)
  starting transfers between devices  10.8 us (3%)
    reduce_scatter x5, waiting for transfers between devices, process(): lax.psum_scatter(lax.cond(active, compute, quiet).astype(jnp.bfloat16), '...  122 us
    ppermute x5, waiting for transfers between devices, partner(): return lax.ppermute(block, axis, route)  45.9 us
    all_gather x5, blocking collectives, process(): incoming_rows = lax.all_gather(local_in, 'tp', axis=0, tiled=True)  36.4 us
    all_gather x5, blocking collectives, process(): full_rows = lax.all_gather(normed[slot], 'tp', axis=0, tiled=True)  33.6 us
    dynamic_slice x16, local copies, waits for them, and re-layouts, process(): store[slot]  21.8 us
    dynamic_update_slice x21, other arithmetic, process(): lax.dynamic_update_index_in_dim(store, jnp.where(active, item, store[slot...  19.9 us
    dot_general x6, matrix products, contract_last(): lax.dot_general(left, right, (((1,), (1,)), ((), ())), preferred_element_...  14 us
    dynamic_update_slice x5, other arithmetic, process(): lax.dynamic_update_index_in_dim(backs, jnp.where(active, back, backs[slot...  9.15 us
  transfers between devices with their start and end apart: 14, of which 9 were waited for; matrix products, arithmetic and copies ran while one was open for 16% of the time, Pallas kernels for 0%

commit v1 on v0

--- a/solution.py
+++ b/solution.py
@@ -1,6 +1,9 @@
+import functools
 import jax
 import jax.numpy as jnp
 from jax import lax
+from jax.experimental import pallas as pl
+from jax.experimental.pallas import tpu as pltpu
 from jax.sharding import PartitionSpec as P
 
 epsilon = 1e-05
@@ -189,9 +192,419 @@
     return (backs[None], new_gate, new_up, new_down)
 
 
+def masks_even(count):
+    return sorted(range(2, count, 2), key=lambda m: -(m & -m))
+
+
+def relay_kernel(
+    n,
+    depth,
+    li_ref,
+    cot_ref,
+    gate_hbm,
+    up_hbm,
+    down_hbm,
+    back_ref,
+    normed_out,
+    incoming_out,
+    hidden_out,
+    gate_out,
+    up_out,
+    gate_w,
+    up_w,
+    down_w,
+    nrm,
+    inc,
+    slope,
+    silu_s,
+    exact_s,
+    inv_s,
+    parts,
+    rs_recv,
+    z_send,
+    load_sem,
+    ssem,
+    rsem,
+):
+    micro, rows, width = li_ref.shape
+    hid = down_w.shape[0]
+    total = n * rows
+    half = width // 2
+    bits = n.bit_length() - 1
+    s = lax.axis_index("segment")
+    t = lax.axis_index("tp")
+    p = lax.div(s, 2)
+    d = lax.rem(s, 2)
+    mirror = s + 1 - 2 * d
+
+    def flip(mask):
+        value = t
+        for b in range(bits):
+            if mask >> b & 1:
+                value = value + (1 << b) * (1 - 2 * lax.rem(lax.div(t, 1 << b), 2))
+        return value
+
+    def copy(k, kind, slot, src, dst, device):
+        return pltpu.make_async_remote_copy(
+            src_ref=src,
+            dst_ref=dst,
+            send_sem=ssem.at[k, kind * n + slot],
+            recv_sem=rsem.at[k, kind * n + slot],
+            device_id=device,
+            device_id_type=pl.DeviceIdType.MESH,
+        )
+
+    loads = [
+        pltpu.make_async_copy(a, b, load_sem.at[i])
+        for i, (a, b) in enumerate(((gate_hbm, gate_w), (up_hbm, up_w), (down_hbm, down_w)))
+    ]
+    for load in loads:
+        load.start()
+
+    barrier = pltpu.get_barrier_semaphore()
+
+    def greet(device):
+        pl.semaphore_signal(
+            barrier, inc=1, device_id=device, device_id_type=pl.DeviceIdType.MESH
+        )
+
+    for b in range(bits):
+        greet({"tp": flip(1 << b)})
+    greet({"segment": mirror})
+
+    @pl.when(p > 0)
+    def _():
+        greet({"segment": s - 2})
+
+    @pl.when(p < depth - 1)
+    def _():
+        greet({"segment": s + 2})
+
+    for k in range(micro):
+        x = li_ref[k].astype(jnp.float32)
+        inv = lax.rsqrt(jnp.mean(x * x, axis=-1, keepdims=True) + epsilon)
+        exact = x * inv
+        inv_s[k] = inv
+        exact_s[k] = exact
+        nrm[0, k, t] = exact.astype(jnp.bfloat16)
+
+    peers = bits + 1 + jnp.minimum(p, 1) + jnp.minimum(depth - 1 - p, 1)
+    pl.semaphore_wait(barrier, peers)
+
+    def ag_copy(kind, k, m, b):
+        buf = (nrm, inc)[kind]
+        block = buf.at[0, k, flip(m)]
+        return copy(k, kind, m | 1 << b, block, block, {"tp": flip(1 << b)})
+
+    def ag_arrival(kind, k, slot):
+        buf = (nrm, inc)[kind]
+        block = buf.at[0, k, flip(slot)]
+        low = slot & -slot
+        return copy(k, kind, slot, block, block, {"tp": flip(low)})
+
+    def ag_start(kind, k):
+        for b in reversed(range(bits)):
+            ag_copy(kind, k, 0, b).start()
+
+    def ag_forward(kind, k):
+        for m in masks_even(n):
+            ag_arrival(kind, k, m).wait_recv()
+            for b in reversed(range(bits)):
+                if 1 << b < (m & -m):
+                    ag_copy(kind, k, m, b).start()
+
+    def ag_finish(kind, k):
+        for m in range(1, n, 2):
+            ag_arrival(kind, k, m).wait_recv()
+
+    def mirror_copy(kind, k):
+        buf = (nrm, inc)[kind]
+        return copy(k, kind, 0, buf.at[0, k], buf.at[1, k], {"segment": mirror})
+
+    def forward(side, k):
+        start = (side * micro + k) * total
+        lhs = nrm[side, k].reshape(total, width)
+        step = min(256, hid)
+
+        @pl.loop(0, hid // step)
+        def _(j):
+            cols = pl.ds(pl.multiple_of(j * step, step), step)
+            g = jnp.dot(lhs, gate_w[:, cols], preferred_element_type=jnp.float32)
+            u = jnp.dot(lhs, up_w[:, cols], preferred_element_type=jnp.float32)
+            sigma = jax.nn.sigmoid(g)
+            sl = g * sigma
+            hidden_out[start : start + total, cols] = (sl * u).astype(jnp.bfloat16)
+            slope[start : start + total, cols] = u * sigma * (1.0 + g * (1.0 - sigma))
+            silu_s[start : start + total, cols] = sl
+
+        keep = pl.ds(pl.multiple_of(d * half, half), half)
+        normed_out[start : start + total, :] = nrm[side, k, :, :, keep].reshape(total, half)
+
+    def factors(side, k):
+        start = (side * micro + k) * total
+        lhs = inc[side, k].reshape(total, width)
+        step = min(256, hid)
+
+        @pl.loop(0, hid // step)
+        def _(j):
+            cols = pl.ds(pl.multiple_of(j * step, step), step)
+            grad = contract_last(lhs, down_w[cols, :])
+            gate_out[start : start + total, cols] = (
+                grad * slope[start : start + total, cols]
+            ).astype(jnp.bfloat16)
+            up_out[start : start + total, cols] = (
+                grad * silu_s[start : start + total, cols]
+            ).astype(jnp.bfloat16)
+
+    def keep_incoming(side, k):
+        start = (side * micro + k) * total
+        keep = pl.ds(pl.multiple_of(d * half, half), half)
+        incoming_out[start : start + total, :] = inc[side, k, :, :, keep].reshape(total, half)
+
+    def partial_grads(k):
+        start = k * total
+        gg = gate_out[start : start + total, :]
+        ug = up_out[start : start + total, :]
+        step = min(256, width)
+
+        @pl.loop(0, width // step)
+        def _(j):
+            cols = pl.ds(pl.multiple_of(j * step, step), step)
+            part = contract_last(gg, gate_w[cols, :]) + contract_last(ug, up_w[cols, :])
+            parts[k, :, :, cols] = part.astype(jnp.bfloat16).reshape(n, rows, step)
+
+    def rs_copy(k, b, m):
+        q = m | 1 << b
+        return copy(k, 2, q, parts.at[k, flip(q)], rs_recv.at[k, q], {"tp": flip(1 << b)})
+
+    def rs_round(k, b):
+        for m in range(0, n, 1 << (b + 1)):
+            q = m | 1 << b
+            if b:
+                value = parts[k, flip(q)].astype(jnp.float32)
+                for lower in range(b):
+                    value = value + rs_recv[k, q | 1 << lower].astype(jnp.float32)
+                parts[k, flip(q)] = value.astype(jnp.bfloat16)
+            rs_copy(k, b, m).start()
+
+    def rs_wait(k, b):
+        for m in range(0, n, 1 << (b + 1)):
+            rs_copy(k, b, m).wait_recv()
+
+    def z_copy(k):
+        return copy(k, 2, 0, z_send.at[k], inc.at[0, k, t], {"segment": s + 2})
+
+    def z_arrival(k):
+        return copy(k, 2, 0, z_send.at[k], inc.at[0, k, t], {"segment": s - 2})
+
+    def finish(k):
+        value = parts[k, t].astype(jnp.float32)
+        for b in range(bits):
+            value = value + rs_recv[k, 1 << b].astype(jnp.float32)
+        base = exact_s[k]
+        back = inc[0, k, t].astype(jnp.float32) + inv_s[k] * (
+            value - base * jnp.mean(value * base, axis=-1, keepdims=True)
+        )
+        back = back.astype(jnp.bfloat16)
+        z_send[k] = back
+
+        @pl.when(p < depth - 1)
+        def _():
+            z_copy(k).start()
+
+        back_ref[k] = back
+
+    first = p == 0
+    early = p * 2 >= depth
+
+    for k in range(micro):
+        ag_start(0, k)
+
+        @pl.when(first)
+        def _():
+            inc[0, k, t] = cot_ref[d, k]
+            ag_start(1, k)
+
+    def mirror_forward():
+        for k in range(micro):
+            mirror_copy(0, k).wait_recv()
+            forward(1, k)
+
+    for k in range(micro):
+        ag_forward(0, k)
+
+        @pl.when(first)
+        def _():
+            ag_forward(1, k)
+
+        ag_finish(0, k)
+        mirror_copy(0, k).start()
+        if k == 0:
+            loads[0].wait()
+            loads[1].wait()
+            forward(0, k)
+        if k == 0:
+            loads[2].wait()
+
+    @pl.when(jnp.logical_not(first))
+    def _():
+        for k in range(1, micro):
+            forward(0, k)
+
+    @pl.when(early)
+    def _():
+        mirror_forward()
+
+    def receive(k):
+        @pl.when(jnp.logical_not(first))
+        def _():
+            z_arrival(k).wait_recv()
+            ag_start(1, k)
+
+    def relay(k):
+        @pl.when(jnp.logical_not(first))
+        def _():
+            ag_forward(1, k)
+
+    def compute(k):
+        ag_finish(1, k)
+        mirror_copy(1, k).start()
+        factors(0, k)
+        partial_grads(k)
+        rs_round(k, 0)
+        keep_incoming(0, k)
+
+    def reduce(k):
+        for b in range(1, bits):
+            rs_wait(k, b - 1)
+            rs_round(k, b)
+
+    def end(k):
+        rs_wait(k, bits - 1)
+        finish(k)
+
+    def mirror_factors(k):
+        mirror_copy(1, k).wait_recv()
+        factors(1, k)
+        keep_incoming(1, k)
+
+    receive(0)
+    relay(0)
+    compute(0)
+
+    @pl.when(first)
+    def _():
+        for k in range(1, micro):
+            forward(0, k)
+
+    for k in range(1, micro):
+        receive(k)
+        reduce(k - 1)
+        relay(k)
+        end(k - 1)
+        compute(k)
+    reduce(micro - 1)
+
+    @pl.when(early)
+    def _():
+        for k in range(micro - 1):
+            mirror_factors(k)
+
+    end(micro - 1)
+
+    @pl.when(jnp.logical_not(early))
+    def _():
+        mirror_forward()
+        for k in range(micro - 1):
+            mirror_factors(k)
+
+    mirror_factors(micro - 1)
+
+    for k in range(micro):
+        for kind in range(2):
+            mirror_copy(kind, k).wait_send()
+            for b in range(bits):
+                for m in range(0, n, 1 << (b + 1)):
+                    ag_copy(kind, k, m, b).wait_send()
+        for b in range(bits):
+            for m in range(0, n, 1 << (b + 1)):
+                rs_copy(k, b, m).wait_send()
+
+        @pl.when(p < depth - 1)
+        def _():
+            z_copy(k).wait_send()
+
+
+def relayed(
+    segments,
+    n,
+    layer_inputs,
+    cotangent,
+    gate_weight,
+    up_weight,
+    down_weight,
+    gate_momentum,
+    up_momentum,
+    down_momentum,
+):
+    _, micro, rows, width = layer_inputs.shape
+    hid = gate_weight.shape[2]
+    half = width // 2
+    flat = 2 * micro * n * rows
+    vmem = pl.BlockSpec(memory_space=pltpu.VMEM)
+    hbm = pl.BlockSpec(memory_space=pl.ANY)
+    bf, f32 = jnp.bfloat16, jnp.float32
+    back, normed, incoming, hidden, gate, up = pl.pallas_call(
+        functools.partial(relay_kernel, n, segments // 2),
+        name="relay",
+        out_shape=(
+            jax.ShapeDtypeStruct((micro, rows, width), bf),
+            jax.ShapeDtypeStruct((flat, half), bf),
+            jax.ShapeDtypeStruct((flat, half), bf),
+            jax.ShapeDtypeStruct((flat, hid), bf),
+            jax.ShapeDtypeStruct((flat, hid), bf),
+            jax.ShapeDtypeStruct((flat, hid), bf),
+        ),
+        in_specs=[vmem, vmem, hbm, hbm, hbm],
+        out_specs=(vmem,) * 6,
+        scratch_shapes=[
+            pltpu.VMEM((width, hid), bf),
+            pltpu.VMEM((width, hid), bf),
+            pltpu.VMEM((hid, width), bf),
+            pltpu.VMEM((2, micro, n, rows, width), bf),
+            pltpu.VMEM((2, micro, n, rows, width), bf),
+            pltpu.VMEM((flat, hid), f32),
+            pltpu.VMEM((flat, hid), f32),
+            pltpu.VMEM((micro, rows, width), f32),
+            pltpu.VMEM((micro, rows, 1), f32),
+            pltpu.VMEM((micro, n, rows, width), bf),
+            pltpu.VMEM((micro, n, rows, width), bf),
+            pltpu.VMEM((micro, rows, width), bf),
+            pltpu.SemaphoreType.DMA((3,)),
+            pltpu.SemaphoreType.DMA((micro, 3 * n)),
+            pltpu.SemaphoreType.DMA((micro, 3 * n)),
+        ],
+        compiler_params=pltpu.CompilerParams(
+            collective_id=0, has_side_effects=True, vmem_limit_bytes=56 << 20
+        ),
+    )(layer_inputs[0], cotangent, gate_weight[0], up_weight[0], down_weight[0])
+    new_gate = momentum_decay * gate_momentum[0] + contract_rows(normed, gate)
+    new_up = momentum_decay * up_momentum[0] + contract_rows(normed, up)
+    new_down = momentum_decay * down_momentum[0] + contract_rows(hidden, incoming)
+    return (back[None], new_gate[None], new_up[None], new_down[None])
+
+
+def choose(segments, n, *arrays):
+    rows = arrays[0].shape[2]
+    if rows % 16 == 0 and n > 1 and n & (n - 1) == 0:
+        return relayed(segments, n, *arrays)
+    return shards(*arrays)
+
+
 def solution(mesh):
+    body = functools.partial(choose, mesh.shape["segment"], mesh.shape["tp"])
     return jax.shard_map(
-        shards,
+        body,
         mesh=mesh,
         in_specs=(
             P("segment", None, "tp", None),

time: 397 us -> 131 us (0.33)
  waiting for transfers between devices: 168 us -> 0 us
  Pallas kernels: 0 us -> 117 us
  blocking collectives: 70 us -> 0 us
  other arithmetic: 53.3 us -> 0 us
  local copies, waits for them, and re-layouts: 47 us -> 1.32 us
  matrix products: 29.2 us -> 11.7 us
  between operations: 13.9 us -> 0.71 us
  starting transfers between devices: 10.8 us -> 0 us
    reduce_scatter x5 -> x0, waiting for transfers between devices: 122 us -> none  [process(): lax.psum_scatter(lax.cond(active, compute, quiet).astype(jnp.bfloat16), '...]
    pallas_call x0 -> x1, Pallas kernels: none -> 117 us  [relayed(): pl.pallas_call(functools.partial(relay_kernel, n, segments // 2), name='r...]
    all_gather x10 -> x0, blocking collectives: 70 us -> none  [the longest x5 36.4 us: process(): incoming_rows = lax.all_gather(local_in, 'tp', axis=0, tiled=True)]
    ppermute x9 -> x0, waiting for transfers between devices: 46 us -> none  [the longest x5 45.9 us: partner(): return lax.ppermute(block, axis, route)]
    dynamic_slice x27 -> x0, local copies, waits for them, and re-layouts: 32.7 us -> none  [the longest x16 21.8 us: process(): store[slot]]
    dynamic_update_slice x26 -> x0, other arithmetic: 29 us -> none  [the longest x21 19.9 us: process(): lax.dynamic_update_index_in_dim(store, jnp.where(active, item, store[slot...]
    dot_general x10 -> x0, matrix products: 21.6 us -> none  [the longest x6 14 us: contract_last(): lax.dot_general(left, right, (((1,), (1,)), ((), ())), preferred_element_...]
    broadcast_in_dim x3 -> x0, other arithmetic: 10.8 us -> none  [the longest x1 3.61 us: shards(): new_gate = (momentum_decay * gate_momentum[0] + gate_share)[None]]
  transfers between devices with their start and end apart: 14 -> 0, of which waited for: 9 -> 0; matrix products, arithmetic and copies ran while one was open for 16% -> 0% of each run, Pallas kernels for 0% -> 0%
where the time goes in v1:
time: 131 us
  Pallas kernels  117 us (89%)
  matrix products  11.7 us (9%)
  local copies, waits for them, and re-layouts  1.32 us (1%)
    pallas_call x1, Pallas kernels, relayed(): pl.pallas_call(functools.partial(relay_kernel, n, segments // 2), name='r...  117 us
    dot_general x3, matrix products, contract_rows(): lax.dot_general(left, right, (((0,), (0,)), ((), ())), preferred_element_...  11.7 us

profile of v1, /device:TPU:24, one launch (start us, length us, event | category | flops | bytes accessed | tf_op | source)
XLA Modules:
  0.0 130.6 jit_solution(484966995456401045)
XLA Ops:
  0.6 0.0 copy-start.1
  0.6 116.8 %relay.1 = (bf16[2,32,2048]{2,1,0:T(8,128)(2,1)}, bf16[512,1024]{1,0:T(8,128)(2,1)}, bf16[512,1024]{1,0:T(8,128)(2,1)}, bf16[512,1024]{1,0:T(8,128)(2,1)}, bf16[...) custom-call(bf16[2,32,2048]{2,1,0:T(8,128)(2,1)} %bitcast.32, bf16[2,2,32,2048]{3,2,1,0:T(8,128)(2,1)} %cot_ref.1, ...), custom_call_target="tpu_custom_call" | custom-call | tf_op jit(solution)/shard_map/relay/pallas_call | solution.py:557
  117.4 0.0 copy-done.1
  117.4 0.0 copy-start
  117.5 0.0 copy-start.2
  117.5 0.0 copy-start.6
  117.5 5.0 %fusion.2 = f32[1,1024,1024]{2,1,0:T(8,128)} fusion(f32[1,1024,1024]{2,1,0:T(8,128)S(1)} %copy-done.1, bf16[512,1024]{1,0:T(8,128)(2,1)} %get-tuple-element.11, bf16[512,1024]{1,0:T(8,128)(2,1)} %get-tuple-element.12), kind=kOutput, calls=%fused_computation.5 | convolution fusion | flops 1075838976 | bytes 10485760 | tf_op jit(solution)/shard_map/dot_general | solution.py:36
  122.5 0.0 copy-done
  122.5 0.0 copy-done.2
  122.5 0.0 copy-done.6
  122.5 0.0 copy-start.3
  122.5 0.0 copy-start.4
  122.5 0.0 copy-start.5
  122.5 3.4 %fusion.1 = f32[1,1024,1024]{2,1,0:T(8,128)} fusion(f32[1,1024,1024]{2,1,0:T(8,128)S(1)} %copy-done.2, bf16[512,1024]{1,0:T(8,128)(2,1)S(1)} %copy-done, bf16[512,1024]{1,0:T(8,128)(2,1)S(1)} %copy-done.6), kind=kOutput, calls=%fused_computation.3 | convolution fusion | flops 1075838976 | bytes 10485760 | tf_op jit(solution)/shard_map/dot_general | solution.py:36
  125.9 0.0 copy-done.3
  125.9 0.0 copy-done.4
  125.9 0.6 copy-done.5
  126.5 0.0 copy-start.7
  126.5 3.4 %fusion = f32[1,1024,1024]{2,1,0:T(8,128)} fusion(f32[1,1024,1024]{2,1,0:T(8,128)S(1)} %copy-done.3, bf16[512,1024]{1,0:T(8,128)(2,1)S(1)} %copy-done.4, bf16[512,1024]{1,0:T(8,128)(2,1)S(1)} %copy-done.5), kind=kOutput, calls=%fused_computation.1 | convolution fusion | flops 1075838976 | bytes 10485760 | tf_op jit(solution)/shard_map/dot_general | solution.py:36
  129.8 0.0 copy-done.7
  129.8 0.7 copy.13
Async XLA Ops:
  0.6 116.8 %copy-start.1 = (f32[1,1024,1024]{2,1,0:T(8,128)S(1)}, f32[1,1024,1024]{2,1,0:T(8,128)}, u32[]{:S(2)}) copy-start(f32[1,1024,1024]{2,1,0:T(8,128)} %param.13) | copy-start | bytes 12582916
  117.4 5.0 %copy-start = (bf16[512,1024]{1,0:T(8,128)(2,1)S(1)}, bf16[512,1024]{1,0:T(8,128)(2,1)}, u32[]{:S(2)}) copy-start(bf16[512,1024]{1,0:T(8,128)(2,1)} %get-tuple-element.11) | copy-start | bytes 3145732
  117.5 5.0 %copy-start.2 = (f32[1,1024,1024]{2,1,0:T(8,128)S(1)}, f32[1,1024,1024]{2,1,0:T(8,128)}, u32[]{:S(2)}) copy-start(f32[1,1024,1024]{2,1,0:T(8,128)} %param.14) | copy-start | bytes 12582916
  117.5 5.0 %copy-start.6 = (bf16[512,1024]{1,0:T(8,128)(2,1)S(1)}, bf16[512,1024]{1,0:T(8,128)(2,1)}, u32[]{:S(2)}) copy-start(bf16[512,1024]{1,0:T(8,128)(2,1)} %get-tuple-element.13) | copy-start | bytes 3145732
  122.5 3.4 %copy-start.3 = (f32[1,1024,1024]{2,1,0:T(8,128)S(1)}, f32[1,1024,1024]{2,1,0:T(8,128)}, u32[]{:S(2)}) copy-start(f32[1,1024,1024]{2,1,0:T(8,128)} %param.15) | copy-start | bytes 12582916
  122.5 3.4 %copy-start.4 = (bf16[512,1024]{1,0:T(8,128)(2,1)S(1)}, bf16[512,1024]{1,0:T(8,128)(2,1)}, u32[]{:S(2)}) copy-start(bf16[512,1024]{1,0:T(8,128)(2,1)} %get-tuple-element.14) | copy-start | bytes 3145732
  122.5 4.0 %copy-start.5 = (bf16[512,1024]{1,0:T(8,128)(2,1)S(1)}, bf16[512,1024]{1,0:T(8,128)(2,1)}, u32[]{:S(2)}) copy-start(bf16[512,1024]{1,0:T(8,128)(2,1)} %get-tuple-element.15) | copy-start | bytes 3145732
  126.5 3.4 %copy-start.7 = (bf16[2,32,2048]{2,1,0:T(8,128)(2,1)S(1)}, bf16[2,32,2048]{2,1,0:T(8,128)(2,1)}, u32[]{:S(2)}) copy-start(bf16[2,32,2048]{2,1,0:T(8,128)(2,1)} %get-tuple-element.10) | copy-start | bytes 786436

commit v2 on v1

--- a/solution.py
+++ b/solution.py
@@ -222,6 +222,9 @@
     parts,
     rs_recv,
     z_send,
+    gate_t,
+    up_t,
+    down_t,
     load_sem,
     ssem,
     rsem,
@@ -231,6 +234,8 @@
     total = n * rows
     half = width // 2
     bits = n.bit_length() - 1
+    pieces = ssem.shape[1]
+    size = rows // pieces
     s = lax.axis_index("segment")
     t = lax.axis_index("tp")
     p = lax.div(s, 2)
@@ -244,12 +249,15 @@
                 value = value + (1 << b) * (1 - 2 * lax.rem(lax.div(t, 1 << b), 2))
         return value
 
-    def copy(k, kind, slot, src, dst, device):
+    def piece(c):
+        return pl.ds(c * size, size)
+
+    def copy(k, c, kind, slot, src, dst, device):
         return pltpu.make_async_remote_copy(
             src_ref=src,
             dst_ref=dst,
-            send_sem=ssem.at[k, kind * n + slot],
-            recv_sem=rsem.at[k, kind * n + slot],
+            send_sem=ssem.at[k, c, kind * n + slot],
+            recv_sem=rsem.at[k, c, kind * n + slot],
             device_id=device,
             device_id_type=pl.DeviceIdType.MESH,
         )
@@ -291,35 +299,37 @@
     peers = bits + 1 + jnp.minimum(p, 1) + jnp.minimum(depth - 1 - p, 1)
     pl.semaphore_wait(barrier, peers)
 
-    def ag_copy(kind, k, m, b):
+    def ag_copy(kind, k, c, m, b):
         buf = (nrm, inc)[kind]
-        block = buf.at[0, k, flip(m)]
-        return copy(k, kind, m | 1 << b, block, block, {"tp": flip(1 << b)})
-
-    def ag_arrival(kind, k, slot):
+        block = buf.at[0, k, flip(m), piece(c)]
+        return copy(k, c, kind, m | 1 << b, block, block, {"tp": flip(1 << b)})
+
+    def ag_arrival(kind, k, c, slot):
         buf = (nrm, inc)[kind]
-        block = buf.at[0, k, flip(slot)]
+        block = buf.at[0, k, flip(slot), piece(c)]
         low = slot & -slot
-        return copy(k, kind, slot, block, block, {"tp": flip(low)})
-
-    def ag_start(kind, k):
+        return copy(k, c, kind, slot, block, block, {"tp": flip(low)})
+
+    def ag_start(kind, k, c):
         for b in reversed(range(bits)):
-            ag_copy(kind, k, 0, b).start()
+            ag_copy(kind, k, c, 0, b).start()
 
     def ag_forward(kind, k):
-        for m in masks_even(n):
-            ag_arrival(kind, k, m).wait_recv()
-            for b in reversed(range(bits)):
-                if 1 << b < (m & -m):
-                    ag_copy(kind, k, m, b).start()
+        for c in range(pieces):
+            for m in masks_even(n):
+                ag_arrival(kind, k, c, m).wait_recv()
+                for b in reversed(range(bits)):
+                    if 1 << b < (m & -m):
+                        ag_copy(kind, k, c, m, b).start()
 
     def ag_finish(kind, k):
-        for m in range(1, n, 2):
-            ag_arrival(kind, k, m).wait_recv()
+        for c in range(pieces):
+            for m in range(1, n, 2):
+                ag_arrival(kind, k, c, m).wait_recv()
 
     def mirror_copy(kind, k):
         buf = (nrm, inc)[kind]
-        return copy(k, kind, 0, buf.at[0, k], buf.at[1, k], {"segment": mirror})
+        return copy(k, 0, kind, 0, buf.at[0, k], buf.at[1, k], {"segment": mirror})
 
     def forward(side, k):
         start = (side * micro + k) * total
@@ -340,15 +350,18 @@
         keep = pl.ds(pl.multiple_of(d * half, half), half)
         normed_out[start : start + total, :] = nrm[side, k, :, :, keep].reshape(total, half)
 
-    def factors(side, k):
+    def factors(side, k, turned):
         start = (side * micro + k) * total
         lhs = inc[side, k].reshape(total, width)
-        step = min(256, hid)
+        step = min(512, hid)
 
         @pl.loop(0, hid // step)
         def _(j):
             cols = pl.ds(pl.multiple_of(j * step, step), step)
-            grad = contract_last(lhs, down_w[cols, :])
+            if turned:
+                grad = jnp.dot(lhs, down_t[:, cols], preferred_element_type=jnp.float32)
+            else:
+                grad = contract_last(lhs, down_w[cols, :])
             gate_out[start : start + total, cols] = (
                 grad * slope[start : start + total, cols]
             ).astype(jnp.bfloat16)
@@ -361,69 +374,83 @@
         keep = pl.ds(pl.multiple_of(d * half, half), half)
         incoming_out[start : start + total, :] = inc[side, k, :, :, keep].reshape(total, half)
 
-    def partial_grads(k):
+    def partial_grads(k, turned):
         start = k * total
-        gg = gate_out[start : start + total, :]
-        ug = up_out[start : start + total, :]
-        step = min(256, width)
+        step = min(512, width)
 
         @pl.loop(0, width // step)
         def _(j):
+            gg = gate_out[start : start + total, :]
+            ug = up_out[start : start + total, :]
             cols = pl.ds(pl.multiple_of(j * step, step), step)
-            part = contract_last(gg, gate_w[cols, :]) + contract_last(ug, up_w[cols, :])
+            if turned:
+                part = jnp.dot(gg, gate_t[:, cols], preferred_element_type=jnp.float32)
+                part = part + jnp.dot(ug, up_t[:, cols], preferred_element_type=jnp.float32)
+            else:
+                part = contract_last(gg, gate_w[cols, :]) + contract_last(ug, up_w[cols, :])
             parts[k, :, :, cols] = part.astype(jnp.bfloat16).reshape(n, rows, step)
 
-    def rs_copy(k, b, m):
+    def turn(source, target):
+        step = 256
+
+        @pl.loop(0, source.shape[1] // step)
+        def _(j):
+            cols = pl.ds(pl.multiple_of(j * step, step), step)
+            target[cols, :] = source[:, cols].T
+
+    def rs_copy(k, c, b, m):
         q = m | 1 << b
-        return copy(k, 2, q, parts.at[k, flip(q)], rs_recv.at[k, q], {"tp": flip(1 << b)})
-
-    def rs_round(k, b):
+        src = parts.at[k, flip(q), piece(c)]
+        return copy(k, c, 2, q, src, rs_recv.at[k, q, piece(c)], {"tp": flip(1 << b)})
+
+    def rs_round(k, c, b):
         for m in range(0, n, 1 << (b + 1)):
             q = m | 1 << b
             if b:
-                value = parts[k, flip(q)].astype(jnp.float32)
+                value = parts[k, flip(q), piece(c)].astype(jnp.float32)
                 for lower in range(b):
-                    value = value + rs_recv[k, q | 1 << lower].astype(jnp.float32)
-                parts[k, flip(q)] = value.astype(jnp.bfloat16)
-            rs_copy(k, b, m).start()
-
-    def rs_wait(k, b):
+                    value = value + rs_recv[k, q | 1 << lower, piece(c)].astype(jnp.float32)
+                parts[k, flip(q), piece(c)] = value.astype(jnp.bfloat16)
+            rs_copy(k, c, b, m).start()
+
+    def rs_wait(k, c, b):
         for m in range(0, n, 1 << (b + 1)):
-            rs_copy(k, b, m).wait_recv()
-
-    def z_copy(k):
-        return copy(k, 2, 0, z_send.at[k], inc.at[0, k, t], {"segment": s + 2})
-
-    def z_arrival(k):
-        return copy(k, 2, 0, z_send.at[k], inc.at[0, k, t], {"segment": s - 2})
-
-    def finish(k):
-        value = parts[k, t].astype(jnp.float32)
+            rs_copy(k, c, b, m).wait_recv()
+
+    def z_copy(k, c, step=2):
+        dst = inc.at[0, k, t, piece(c)]
+        return copy(k, c, 2, 0, z_send.at[k, piece(c)], dst, {"segment": s + step})
+
+    def finish(k, c):
+        span = piece(c)
+        value = parts[k, t, span].astype(jnp.float32)
         for b in range(bits):
-            value = value + rs_recv[k, 1 << b].astype(jnp.float32)
-        base = exact_s[k]
-        back = inc[0, k, t].astype(jnp.float32) + inv_s[k] * (
+            value = value + rs_recv[k, 1 << b, span].astype(jnp.float32)
+        base = exact_s[k, span]
+        back = inc[0, k, t, span].astype(jnp.float32) + inv_s[k, span] * (
             value - base * jnp.mean(value * base, axis=-1, keepdims=True)
         )
         back = back.astype(jnp.bfloat16)
-        z_send[k] = back
+        z_send[k, span] = back
 
         @pl.when(p < depth - 1)
         def _():
-            z_copy(k).start()
-
-        back_ref[k] = back
+            z_copy(k, c).start()
+
+        back_ref[k, span] = back
 
     first = p == 0
     early = p * 2 >= depth
 
     for k in range(micro):
-        ag_start(0, k)
+        for c in range(pieces):
+            ag_start(0, k, c)
 
         @pl.when(first)
         def _():
             inc[0, k, t] = cot_ref[d, k]
-            ag_start(1, k)
+            for c in range(pieces):
+                ag_start(1, k, c)
 
     def mirror_forward():
         for k in range(micro):
@@ -448,6 +475,9 @@
 
     @pl.when(jnp.logical_not(first))
     def _():
+        turn(down_w, down_t)
+        turn(gate_w, gate_t)
+        turn(up_w, up_t)
         for k in range(1, micro):
             forward(0, k)
 
@@ -458,8 +488,9 @@
     def receive(k):
         @pl.when(jnp.logical_not(first))
         def _():
-            z_arrival(k).wait_recv()
-            ag_start(1, k)
+            for c in range(pieces):
+                z_copy(k, c, -2).wait_recv()
+                ag_start(1, k, c)
 
     def relay(k):
         @pl.when(jnp.logical_not(first))
@@ -469,23 +500,35 @@
     def compute(k):
         ag_finish(1, k)
         mirror_copy(1, k).start()
-        factors(0, k)
-        partial_grads(k)
-        rs_round(k, 0)
+
+        @pl.when(first)
+        def _():
+            factors(0, k, False)
+            partial_grads(k, False)
+
+        @pl.when(jnp.logical_not(first))
+        def _():
+            factors(0, k, True)
+            partial_grads(k, True)
+
+        for c in range(pieces):
+            rs_round(k, c, 0)
         keep_incoming(0, k)
 
     def reduce(k):
         for b in range(1, bits):
-            rs_wait(k, b - 1)
-            rs_round(k, b)
+            for c in range(pieces):
+                rs_wait(k, c, b - 1)
+                rs_round(k, c, b)
 
     def end(k):
-        rs_wait(k, bits - 1)
-        finish(k)
+        for c in range(pieces):
+            rs_wait(k, c, bits - 1)
+            finish(k, c)
 
     def mirror_factors(k):
         mirror_copy(1, k).wait_recv()
-        factors(1, k)
+        factors(1, k, False)
         keep_incoming(1, k)
 
     receive(0)
@@ -498,8 +541,8 @@
             forward(0, k)
 
     for k in range(1, micro):
+        reduce(k - 1)
         receive(k)
-        reduce(k - 1)
         relay(k)
         end(k - 1)
         compute(k)
@@ -523,16 +566,16 @@
     for k in range(micro):
         for kind in range(2):
             mirror_copy(kind, k).wait_send()
+        for c in range(pieces):
             for b in range(bits):
                 for m in range(0, n, 1 << (b + 1)):
-                    ag_copy(kind, k, m, b).wait_send()
-        for b in range(bits):
-            for m in range(0, n, 1 << (b + 1)):
-                rs_copy(k, b, m).wait_send()
-
-        @pl.when(p < depth - 1)
-        def _():
-            z_copy(k).wait_send()
+                    for kind in range(2):
+                        ag_copy(kind, k, c, m, b).wait_send()
+                    rs_copy(k, c, b, m).wait_send()
+
+            @pl.when(p < depth - 1)
+            def _():
+                z_copy(k, c).wait_send()
 
 
 def relayed(
@@ -553,6 +596,7 @@
     flat = 2 * micro * n * rows
     vmem = pl.BlockSpec(memory_space=pltpu.VMEM)
     hbm = pl.BlockSpec(memory_space=pl.ANY)
+    pieces = 2 if rows % 32 == 0 else 1
     bf, f32 = jnp.bfloat16, jnp.float32
     back, normed, incoming, hidden, gate, up = pl.pallas_call(
         functools.partial(relay_kernel, n, segments // 2),
@@ -580,12 +624,15 @@
             pltpu.VMEM((micro, n, rows, width), bf),
             pltpu.VMEM((micro, n, rows, width), bf),
             pltpu.VMEM((micro, rows, width), bf),
+            pltpu.VMEM((hid, width), bf),
+            pltpu.VMEM((hid, width), bf),
+            pltpu.VMEM((width, hid), bf),
             pltpu.SemaphoreType.DMA((3,)),
-            pltpu.SemaphoreType.DMA((micro, 3 * n)),
-            pltpu.SemaphoreType.DMA((micro, 3 * n)),
+            pltpu.SemaphoreType.DMA((micro, pieces, 3 * n)),
+            pltpu.SemaphoreType.DMA((micro, pieces, 3 * n)),
         ],
         compiler_params=pltpu.CompilerParams(
-            collective_id=0, has_side_effects=True, vmem_limit_bytes=56 << 20
+            collective_id=0, has_side_effects=True, vmem_limit_bytes=60 << 20
         ),
     )(layer_inputs[0], cotangent, gate_weight[0], up_weight[0], down_weight[0])
     new_gate = momentum_decay * gate_momentum[0] + contract_rows(normed, gate)

time: 131 us -> 116 us (0.89)
  Pallas kernels: 117 us -> 100 us
    pallas_call x1, Pallas kernels: 117 us -> 100 us  [relayed(): pl.pallas_call(functools.partial(relay_kernel, n, segments // 2), name='r...]
where the time goes in v2:
time: 116 us; the launch traced here: 115 us
  Pallas kernels  100 us (86%)
  matrix products  13 us (11%)
  local copies, waits for them, and re-layouts  1.32 us (1%)
    pallas_call x1, Pallas kernels, relayed(): pl.pallas_call(functools.partial(relay_kernel, n, segments // 2), name='r...  100 us
    dot_general x3, matrix products, contract_rows(): lax.dot_general(left, right, (((0,), (0,)), ((), ())), preferred_element_...  13 us

profile of v2, /device:TPU:24, one launch (start us, length us, event | category | flops | bytes accessed | tf_op | source)
XLA Modules:
  0.0 115.4 jit_solution(1889423805909205614)
XLA Ops:
  0.6 100.3 %relay.1 = (bf16[2,32,2048]{2,1,0:T(8,128)(2,1)}, bf16[512,1024]{1,0:T(8,128)(2,1)}, bf16[512,1024]{1,0:T(8,128)(2,1)}, bf16[512,1024]{1,0:T(8,128)(2,1)}, bf16[...) custom-call(bf16[2,32,2048]{2,1,0:T(8,128)(2,1)} %bitcast.32, bf16[2,2,32,2048]{3,2,1,0:T(8,128)(2,1)} %cot_ref.1, ...), custom_call_target="tpu_custom_call" | custom-call | tf_op jit(solution)/shard_map/relay/pallas_call | solution.py:601
  101.0 0.0 copy-start
  101.0 0.0 copy-start.1
  101.0 0.0 copy-start.5
  101.0 6.3 %fusion.2 = f32[1,1024,1024]{2,1,0:T(8,128)} fusion(f32[1,1024,1024]{2,1,0:T(8,128)} %param.13, bf16[512,1024]{1,0:T(8,128)(2,1)} %get-tuple-element.11, bf16[512,1024]{1,0:T(8,128)(2,1)} %get-tuple-element.12), kind=kOutput, calls=%fused_computation.5 | convolution fusion | flops 1075838976 | bytes 10485760 | tf_op jit(solution)/shard_map/dot_general | solution.py:36
  107.3 0.0 copy-done
  107.3 0.0 copy-done.1
  107.3 0.0 copy-done.5
  107.3 0.0 copy-start.2
  107.3 0.0 copy-start.3
  107.3 0.0 copy-start.4
  107.3 3.4 %fusion.1 = f32[1,1024,1024]{2,1,0:T(8,128)} fusion(f32[1,1024,1024]{2,1,0:T(8,128)S(1)} %copy-done.1, bf16[512,1024]{1,0:T(8,128)(2,1)S(1)} %copy-done, bf16[512,1024]{1,0:T(8,128)(2,1)S(1)} %copy-done.5), kind=kOutput, calls=%fused_computation.3 | convolution fusion | flops 1075838976 | bytes 10485760 | tf_op jit(solution)/shard_map/dot_general | solution.py:36
  110.7 0.0 copy-done.2
  110.7 0.0 copy-done.3
  110.7 0.6 copy-done.4
  111.3 0.0 copy-start.6
  111.3 3.4 %fusion = f32[1,1024,1024]{2,1,0:T(8,128)} fusion(f32[1,1024,1024]{2,1,0:T(8,128)S(1)} %copy-done.2, bf16[512,1024]{1,0:T(8,128)(2,1)S(1)} %copy-done.3, bf16[512,1024]{1,0:T(8,128)(2,1)S(1)} %copy-done.4), kind=kOutput, calls=%fused_computation.1 | convolution fusion | flops 1075838976 | bytes 10485760 | tf_op jit(solution)/shard_map/dot_general | solution.py:36
  114.7 0.0 copy-done.6
  114.7 0.7 copy.13
Async XLA Ops:
  101.0 6.3 %copy-start = (bf16[512,1024]{1,0:T(8,128)(2,1)S(1)}, bf16[512,1024]{1,0:T(8,128)(2,1)}, u32[]{:S(2)}) copy-start(bf16[512,1024]{1,0:T(8,128)(2,1)} %get-tuple-element.11) | copy-start | bytes 3145732
  101.0 6.3 %copy-start.1 = (f32[1,1024,1024]{2,1,0:T(8,128)S(1)}, f32[1,1024,1024]{2,1,0:T(8,128)}, u32[]{:S(2)}) copy-start(f32[1,1024,1024]{2,1,0:T(8,128)} %param.14) | copy-start | bytes 12582916
  101.0 6.3 %copy-start.5 = (bf16[512,1024]{1,0:T(8,128)(2,1)S(1)}, bf16[512,1024]{1,0:T(8,128)(2,1)}, u32[]{:S(2)}) copy-start(bf16[512,1024]{1,0:T(8,128)(2,1)} %get-tuple-element.13) | copy-start | bytes 3145732
  107.3 3.4 %copy-start.2 = (f32[1,1024,1024]{2,1,0:T(8,128)S(1)}, f32[1,1024,1024]{2,1,0:T(8,128)}, u32[]{:S(2)}) copy-start(f32[1,1024,1024]{2,1,0:T(8,128)} %param.15) | copy-start | bytes 12582916
  107.3 3.4 %copy-start.3 = (bf16[512,1024]{1,0:T(8,128)(2,1)S(1)}, bf16[512,1024]{1,0:T(8,128)(2,1)}, u32[]{:S(2)}) copy-start(bf16[512,1024]{1,0:T(8,128)(2,1)} %get-tuple-element.14) | copy-start | bytes 3145732
  107.3 4.0 %copy-start.4 = (bf16[512,1024]{1,0:T(8,128)(2,1)S(1)}, bf16[512,1024]{1,0:T(8,128)(2,1)}, u32[]{:S(2)}) copy-start(bf16[512,1024]{1,0:T(8,128)(2,1)} %get-tuple-element.15) | copy-start | bytes 3145732
  111.3 3.4 %copy-start.6 = (bf16[2,32,2048]{2,1,0:T(8,128)(2,1)S(1)}, bf16[2,32,2048]{2,1,0:T(8,128)(2,1)}, u32[]{:S(2)}) copy-start(bf16[2,32,2048]{2,1,0:T(8,128)(2,1)} %get-tuple-element.10) | copy-start | bytes 786436

commit v3 on v2

--- a/solution.py
+++ b/solution.py
@@ -321,15 +321,33 @@
                 for b in reversed(range(bits)):
                     if 1 << b < (m & -m):
                         ag_copy(kind, k, c, m, b).start()
+                if c == pieces - 1:
+                    mirror_copy(kind, k, m).start()
 
     def ag_finish(kind, k):
         for c in range(pieces):
             for m in range(1, n, 2):
                 ag_arrival(kind, k, c, m).wait_recv()
 
-    def mirror_copy(kind, k):
+    def mirror_copy(kind, k, m):
         buf = (nrm, inc)[kind]
-        return copy(k, 0, kind, 0, buf.at[0, k], buf.at[1, k], {"segment": mirror})
+        block = flip(m)
+        return copy(
+            k, 0, 3 + kind, m, buf.at[0, k, block], buf.at[1, k, block], {"segment": mirror}
+        )
+
+    def pass_copy(kind, k, m, arriving=0):
+        block = (nrm, inc)[kind].at[1, k, flip(m | arriving)]
+        return copy(k, 0, 5 + kind, m, block, block, {"tp": flip(1)})
+
+    def mirror_pass(kind, k):
+        for m in range(0, n, 2):
+            mirror_copy(kind, k, m).wait_recv()
+            pass_copy(kind, k, m).start()
+
+    def mirror_wait(kind, k):
+        for m in range(0, n, 2):
+            pass_copy(kind, k, m, 1).wait_recv()
 
     def forward(side, k):
         start = (side * micro + k) * total
@@ -440,9 +458,9 @@
         back_ref[k, span] = back
 
     first = p == 0
-    early = p * 2 >= depth
-
-    for k in range(micro):
+    early = jnp.logical_and(p > 0, p * 2 >= depth)
+
+    def open_rows(k):
         for c in range(pieces):
             ag_start(0, k, c)
 
@@ -452,12 +470,13 @@
             for c in range(pieces):
                 ag_start(1, k, c)
 
-    def mirror_forward():
-        for k in range(micro):
-            mirror_copy(0, k).wait_recv()
-            forward(1, k)
-
-    for k in range(micro):
+        mirror_copy(0, k, 0).start()
+
+        @pl.when(first)
+        def _():
+            mirror_copy(1, k, 0).start()
+
+    def spread(k):
         ag_forward(0, k)
 
         @pl.when(first)
@@ -465,21 +484,30 @@
             ag_forward(1, k)
 
         ag_finish(0, k)
-        mirror_copy(0, k).start()
-        if k == 0:
-            loads[0].wait()
-            loads[1].wait()
+
+    def mirror_forward():
+        for k in range(micro):
+            mirror_pass(0, k)
+        for k in range(micro):
+            mirror_wait(0, k)
+            forward(1, k)
+
+    for k in range(micro):
+        open_rows(k)
+    spread(0)
+    loads[0].wait()
+    loads[1].wait()
+    forward(0, 0)
+    loads[2].wait()
+
+    @pl.when(jnp.logical_not(first))
+    def _():
+        for k in range(1, micro):
+            spread(k)
             forward(0, k)
-        if k == 0:
-            loads[2].wait()
-
-    @pl.when(jnp.logical_not(first))
-    def _():
         turn(down_w, down_t)
         turn(gate_w, gate_t)
         turn(up_w, up_t)
-        for k in range(1, micro):
-            forward(0, k)
 
     @pl.when(early)
     def _():
@@ -491,6 +519,7 @@
             for c in range(pieces):
                 z_copy(k, c, -2).wait_recv()
                 ag_start(1, k, c)
+            mirror_copy(1, k, 0).start()
 
     def relay(k):
         @pl.when(jnp.logical_not(first))
@@ -499,7 +528,6 @@
 
     def compute(k):
         ag_finish(1, k)
-        mirror_copy(1, k).start()
 
         @pl.when(first)
         def _():
@@ -526,9 +554,9 @@
             rs_wait(k, c, bits - 1)
             finish(k, c)
 
-    def mirror_factors(k):
-        mirror_copy(1, k).wait_recv()
-        factors(1, k, False)
+    def mirror_factors(k, turned):
+        mirror_wait(1, k)
+        factors(1, k, turned)
         keep_incoming(1, k)
 
     receive(0)
@@ -538,6 +566,7 @@
     @pl.when(first)
     def _():
         for k in range(1, micro):
+            spread(k)
             forward(0, k)
 
     for k in range(1, micro):
@@ -545,27 +574,37 @@
         receive(k)
         relay(k)
         end(k - 1)
+        mirror_pass(1, k - 1)
         compute(k)
     reduce(micro - 1)
+    mirror_pass(1, micro - 1)
 
     @pl.when(early)
     def _():
         for k in range(micro - 1):
-            mirror_factors(k)
+            mirror_factors(k, True)
+
+    @pl.when(jnp.logical_and(early, p == depth - 1))
+    def _():
+        mirror_factors(micro - 1, True)
 
     end(micro - 1)
 
+    @pl.when(jnp.logical_and(early, p < depth - 1))
+    def _():
+        mirror_factors(micro - 1, True)
+
     @pl.when(jnp.logical_not(early))
     def _():
         mirror_forward()
-        for k in range(micro - 1):
-            mirror_factors(k)
-
-    mirror_factors(micro - 1)
+        for k in range(micro):
+            mirror_factors(k, False)
 
     for k in range(micro):
         for kind in range(2):
-            mirror_copy(kind, k).wait_send()
+            for m in range(0, n, 2):
+                mirror_copy(kind, k, m).wait_send()
+                pass_copy(kind, k, m).wait_send()
         for c in range(pieces):
             for b in range(bits):
                 for m in range(0, n, 1 << (b + 1)):
@@ -628,8 +667,8 @@
             pltpu.VMEM((hid, width), bf),
             pltpu.VMEM((width, hid), bf),
             pltpu.SemaphoreType.DMA((3,)),
-            pltpu.SemaphoreType.DMA((micro, pieces, 3 * n)),
-            pltpu.SemaphoreType.DMA((micro, pieces, 3 * n)),
+            pltpu.SemaphoreType.DMA((micro, pieces, 7 * n)),
+            pltpu.SemaphoreType.DMA((micro, pieces, 7 * n)),
         ],
         compiler_params=pltpu.CompilerParams(
             collective_id=0, has_side_effects=True, vmem_limit_bytes=60 << 20

time: 116 us -> 110 us (0.948)
  Pallas kernels: 100 us -> 95.1 us
    pallas_call x1, Pallas kernels: 100 us -> 95.1 us  [relayed(): pl.pallas_call(functools.partial(relay_kernel, n, segments // 2), name='r...]
where the time goes in v3:
time: 110 us
  Pallas kernels  95.1 us (86%)
  matrix products  13 us (12%)
  local copies, waits for them, and re-layouts  1.32 us (1%)
    pallas_call x1, Pallas kernels, relayed(): pl.pallas_call(functools.partial(relay_kernel, n, segments // 2), name='r...  95.1 us
    dot_general x3, matrix products, contract_rows(): lax.dot_general(left, right, (((0,), (0,)), ((), ())), preferred_element_...  13 us

profile of v3, /device:TPU:24, one launch (start us, length us, event | category | flops | bytes accessed | tf_op | source)
XLA Modules:
  0.0 110.1 jit_solution(7451583055610149063)
XLA Ops:
  0.6 95.1 %relay.1 = (bf16[2,32,2048]{2,1,0:T(8,128)(2,1)}, bf16[512,1024]{1,0:T(8,128)(2,1)}, bf16[512,1024]{1,0:T(8,128)(2,1)}, bf16[512,1024]{1,0:T(8,128)(2,1)}, bf16[...) custom-call(bf16[2,32,2048]{2,1,0:T(8,128)(2,1)} %bitcast.32, bf16[2,2,32,2048]{3,2,1,0:T(8,128)(2,1)} %cot_ref.1, ...), custom_call_target="tpu_custom_call" | custom-call | tf_op jit(solution)/shard_map/relay/pallas_call | solution.py:640
  95.7 0.0 copy-start
  95.7 0.0 copy-start.1
  95.7 0.0 copy-start.5
  95.7 6.3 %fusion.2 = f32[1,1024,1024]{2,1,0:T(8,128)} fusion(f32[1,1024,1024]{2,1,0:T(8,128)} %param.13, bf16[512,1024]{1,0:T(8,128)(2,1)} %get-tuple-element.11, bf16[512,1024]{1,0:T(8,128)(2,1)} %get-tuple-element.12), kind=kOutput, calls=%fused_computation.5 | convolution fusion | flops 1075838976 | bytes 10485760 | tf_op jit(solution)/shard_map/dot_general | solution.py:36
  102.0 0.0 copy-done
  102.0 0.0 copy-done.1
  102.0 0.0 copy-done.5
  102.0 0.0 copy-start.2
  102.1 0.0 copy-start.3
  102.1 0.0 copy-start.4
  102.1 3.4 %fusion.1 = f32[1,1024,1024]{2,1,0:T(8,128)} fusion(f32[1,1024,1024]{2,1,0:T(8,128)S(1)} %copy-done.1, bf16[512,1024]{1,0:T(8,128)(2,1)S(1)} %copy-done, bf16[512,1024]{1,0:T(8,128)(2,1)S(1)} %copy-done.5), kind=kOutput, calls=%fused_computation.3 | convolution fusion | flops 1075838976 | bytes 10485760 | tf_op jit(solution)/shard_map/dot_general | solution.py:36
  105.4 0.0 copy-done.2
  105.4 0.0 copy-done.3
  105.4 0.6 copy-done.4
  106.0 0.0 copy-start.6
  106.0 3.4 %fusion = f32[1,1024,1024]{2,1,0:T(8,128)} fusion(f32[1,1024,1024]{2,1,0:T(8,128)S(1)} %copy-done.2, bf16[512,1024]{1,0:T(8,128)(2,1)S(1)} %copy-done.3, bf16[512,1024]{1,0:T(8,128)(2,1)S(1)} %copy-done.4), kind=kOutput, calls=%fused_computation.1 | convolution fusion | flops 1075838976 | bytes 10485760 | tf_op jit(solution)/shard_map/dot_general | solution.py:36
  109.4 0.0 copy-done.6
  109.4 0.7 copy.13
Async XLA Ops:
  95.7 6.3 %copy-start = (bf16[512,1024]{1,0:T(8,128)(2,1)S(1)}, bf16[512,1024]{1,0:T(8,128)(2,1)}, u32[]{:S(2)}) copy-start(bf16[512,1024]{1,0:T(8,128)(2,1)} %get-tuple-element.11) | copy-start | bytes 3145732
  95.7 6.3 %copy-start.1 = (f32[1,1024,1024]{2,1,0:T(8,128)S(1)}, f32[1,1024,1024]{2,1,0:T(8,128)}, u32[]{:S(2)}) copy-start(f32[1,1024,1024]{2,1,0:T(8,128)} %param.14) | copy-start | bytes 12582916
  95.7 6.3 %copy-start.5 = (bf16[512,1024]{1,0:T(8,128)(2,1)S(1)}, bf16[512,1024]{1,0:T(8,128)(2,1)}, u32[]{:S(2)}) copy-start(bf16[512,1024]{1,0:T(8,128)(2,1)} %get-tuple-element.13) | copy-start | bytes 3145732
  102.0 3.4 %copy-start.2 = (f32[1,1024,1024]{2,1,0:T(8,128)S(1)}, f32[1,1024,1024]{2,1,0:T(8,128)}, u32[]{:S(2)}) copy-start(f32[1,1024,1024]{2,1,0:T(8,128)} %param.15) | copy-start | bytes 12582916
  102.1 3.4 %copy-start.3 = (bf16[512,1024]{1,0:T(8,128)(2,1)S(1)}, bf16[512,1024]{1,0:T(8,128)(2,1)}, u32[]{:S(2)}) copy-start(bf16[512,1024]{1,0:T(8,128)(2,1)} %get-tuple-element.14) | copy-start | bytes 3145732
  102.1 4.0 %copy-start.4 = (bf16[512,1024]{1,0:T(8,128)(2,1)S(1)}, bf16[512,1024]{1,0:T(8,128)(2,1)}, u32[]{:S(2)}) copy-start(bf16[512,1024]{1,0:T(8,128)(2,1)} %get-tuple-element.15) | copy-start | bytes 3145732
  106.0 3.4 %copy-start.6 = (bf16[2,32,2048]{2,1,0:T(8,128)(2,1)S(1)}, bf16[2,32,2048]{2,1,0:T(8,128)(2,1)}, u32[]{:S(2)}) copy-start(bf16[2,32,2048]{2,1,0:T(8,128)(2,1)} %get-tuple-element.10) | copy-start | bytes 786436

commit v4 on v3

--- a/solution.py
+++ b/solution.py
@@ -371,7 +371,7 @@
     def factors(side, k, turned):
         start = (side * micro + k) * total
         lhs = inc[side, k].reshape(total, width)
-        step = min(512, hid)
+        step = min(1024, hid)
 
         @pl.loop(0, hid // step)
         def _(j):
@@ -394,7 +394,7 @@
 
     def partial_grads(k, turned):
         start = k * total
-        step = min(512, width)
+        step = min(1024, width)
 
         @pl.loop(0, width // step)
         def _(j):
@@ -563,14 +563,14 @@
     relay(0)
     compute(0)
 
-    @pl.when(first)
-    def _():
-        for k in range(1, micro):
+    for k in range(1, micro):
+        reduce(k - 1)
+
+        @pl.when(first)
+        def _():
             spread(k)
             forward(0, k)
 
-    for k in range(1, micro):
-        reduce(k - 1)
         receive(k)
         relay(k)
         end(k - 1)

time: 110 us -> 106 us (0.964)
  Pallas kernels: 95.1 us -> 90.9 us
    pallas_call x1, Pallas kernels: 95.1 us -> 90.9 us  [relayed(): pl.pallas_call(functools.partial(relay_kernel, n, segments // 2), name='r...]
where the time goes in v4:
time: 106 us
  Pallas kernels  90.9 us (86%)
  matrix products  13 us (12%)
  local copies, waits for them, and re-layouts  1.32 us (1%)
    pallas_call x1, Pallas kernels, relayed(): pl.pallas_call(functools.partial(relay_kernel, n, segments // 2), name='r...  90.9 us
    dot_general x3, matrix products, contract_rows(): lax.dot_general(left, right, (((0,), (0,)), ((), ())), preferred_element_...  13 us

profile of v4, /device:TPU:24, one launch (start us, length us, event | category | flops | bytes accessed | tf_op | source)
XLA Modules:
  0.0 105.9 jit_solution(14497722159128803658)
XLA Ops:
  0.6 90.9 %relay.1 = (bf16[2,32,2048]{2,1,0:T(8,128)(2,1)}, bf16[512,1024]{1,0:T(8,128)(2,1)}, bf16[512,1024]{1,0:T(8,128)(2,1)}, bf16[512,1024]{1,0:T(8,128)(2,1)}, bf16[...) custom-call(bf16[2,32,2048]{2,1,0:T(8,128)(2,1)} %bitcast.32, bf16[2,2,32,2048]{3,2,1,0:T(8,128)(2,1)} %cot_ref.1, ...), custom_call_target="tpu_custom_call" | custom-call | tf_op jit(solution)/shard_map/relay/pallas_call | solution.py:640
  91.5 0.0 copy-start
  91.5 0.0 copy-start.1
  91.5 0.0 copy-start.5
  91.6 6.3 %fusion.2 = f32[1,1024,1024]{2,1,0:T(8,128)} fusion(f32[1,1024,1024]{2,1,0:T(8,128)} %param.13, bf16[512,1024]{1,0:T(8,128)(2,1)} %get-tuple-element.11, bf16[512,1024]{1,0:T(8,128)(2,1)} %get-tuple-element.12), kind=kOutput, calls=%fused_computation.5 | convolution fusion | flops 1075838976 | bytes 10485760 | tf_op jit(solution)/shard_map/dot_general | solution.py:36
  97.8 0.0 copy-done
  97.8 0.0 copy-done.1
  97.8 0.0 copy-done.5
  97.8 0.0 copy-start.2
  97.9 0.0 copy-start.3
  97.9 0.0 copy-start.4
  97.9 3.4 %fusion.1 = f32[1,1024,1024]{2,1,0:T(8,128)} fusion(f32[1,1024,1024]{2,1,0:T(8,128)S(1)} %copy-done.1, bf16[512,1024]{1,0:T(8,128)(2,1)S(1)} %copy-done, bf16[512,1024]{1,0:T(8,128)(2,1)S(1)} %copy-done.5), kind=kOutput, calls=%fused_computation.3 | convolution fusion | flops 1075838976 | bytes 10485760 | tf_op jit(solution)/shard_map/dot_general | solution.py:36
  101.2 0.0 copy-done.2
  101.2 0.0 copy-done.3
  101.2 0.6 copy-done.4
  101.8 0.0 copy-start.6
  101.8 3.4 %fusion = f32[1,1024,1024]{2,1,0:T(8,128)} fusion(f32[1,1024,1024]{2,1,0:T(8,128)S(1)} %copy-done.2, bf16[512,1024]{1,0:T(8,128)(2,1)S(1)} %copy-done.3, bf16[512,1024]{1,0:T(8,128)(2,1)S(1)} %copy-done.4), kind=kOutput, calls=%fused_computation.1 | convolution fusion | flops 1075838976 | bytes 10485760 | tf_op jit(solution)/shard_map/dot_general | solution.py:36
  105.2 0.0 copy-done.6
  105.2 0.7 copy.13
Async XLA Ops:
  91.5 6.3 %copy-start = (bf16[512,1024]{1,0:T(8,128)(2,1)S(1)}, bf16[512,1024]{1,0:T(8,128)(2,1)}, u32[]{:S(2)}) copy-start(bf16[512,1024]{1,0:T(8,128)(2,1)} %get-tuple-element.11) | copy-start | bytes 3145732
  91.5 6.3 %copy-start.1 = (f32[1,1024,1024]{2,1,0:T(8,128)S(1)}, f32[1,1024,1024]{2,1,0:T(8,128)}, u32[]{:S(2)}) copy-start(f32[1,1024,1024]{2,1,0:T(8,128)} %param.14) | copy-start | bytes 12582916
  91.5 6.3 %copy-start.5 = (bf16[512,1024]{1,0:T(8,128)(2,1)S(1)}, bf16[512,1024]{1,0:T(8,128)(2,1)}, u32[]{:S(2)}) copy-start(bf16[512,1024]{1,0:T(8,128)(2,1)} %get-tuple-element.13) | copy-start | bytes 3145732
  97.8 3.4 %copy-start.2 = (f32[1,1024,1024]{2,1,0:T(8,128)S(1)}, f32[1,1024,1024]{2,1,0:T(8,128)}, u32[]{:S(2)}) copy-start(f32[1,1024,1024]{2,1,0:T(8,128)} %param.15) | copy-start | bytes 12582916
  97.9 3.4 %copy-start.3 = (bf16[512,1024]{1,0:T(8,128)(2,1)S(1)}, bf16[512,1024]{1,0:T(8,128)(2,1)}, u32[]{:S(2)}) copy-start(bf16[512,1024]{1,0:T(8,128)(2,1)} %get-tuple-element.14) | copy-start | bytes 3145732
  97.9 4.0 %copy-start.4 = (bf16[512,1024]{1,0:T(8,128)(2,1)S(1)}, bf16[512,1024]{1,0:T(8,128)(2,1)}, u32[]{:S(2)}) copy-start(bf16[512,1024]{1,0:T(8,128)(2,1)} %get-tuple-element.15) | copy-start | bytes 3145732
  101.8 3.4 %copy-start.6 = (bf16[2,32,2048]{2,1,0:T(8,128)(2,1)S(1)}, bf16[2,32,2048]{2,1,0:T(8,128)(2,1)}, u32[]{:S(2)}) copy-start(bf16[2,32,2048]{2,1,0:T(8,128)(2,1)} %get-tuple-element.10) | copy-start | bytes 786436
